TPU v7x, 32 devices: a whole 2x2x4 slice. The times are simulated.
32 devices in a mesh: samp: 8 (over y, x, core), feat: 4 (over z).
Axes of the slice: x: 2, y: 2, z: 4, core: 2. Of those that a mesh axis runs over, the one named last changes fastest.
Arguments:
- points: bfloat16 [4096, 128], P('samp'), may hold values from -6 to 6
- frequencies: bfloat16 [128, 16384], P(None, 'feat'), may hold values from -0.5 to 0.5
- phases: float32 [16384], P('feat'), may hold values from -3.140625 to 3.140625
- signs: int32 [4096], P('samp'), may hold values from -1 to 1, as said below
- picks: int32 [128], P('samp'), may hold values from 0 to 4095, as said below
Outputs:
- gram: float32 [16384, 16384], P('feat', 'samp')
Inputs may be any that keep to these rules, and one draw needn't show every extreme that they name: `signs`: each entry is +1 or -1. `picks`: entry k names a row between (k // 16) * 512 and (k // 16 + 1) * 512 - 1; no row is named twice.
All inputs are finite; a program needn't handle non-finite values.
Results may differ from a plain program's by a relative error of at most 0.0009.
Values may be sent and summed in bfloat16 or wider, within the bound.
A program may use at most 128 MiB of HBM per device.

v0:
```python
import jax
import jax.numpy as jnp
from jax import lax
from jax.sharding import PartitionSpec as P


def partner_2(array, axis, distance):
    return lax.ppermute(array, axis, [(i, i ^ 1 << distance) for i in range(lax.axis_size(axis))])


def from_root(value, axis, source):
    kept = jnp.where(lax.axis_index(axis) == source, value, 0).astype(value.dtype)
    return lax.psum(kept, axis)


def hadamard(order):
    table = jnp.ones((1, 1), jnp.float32)
    for level in range(order.bit_length() - 1):
        table = jnp.concatenate(
            [jnp.concatenate([table, table], 1), jnp.concatenate([table, -table], 1)], 0
        )
    return table


def per_device(points, frequencies, phases, signs, picks):
    rows = points.shape[0]
    width = frequencies.shape[1]
    groups = lax.axis_size("samp")
    blocks = lax.axis_size("feat")
    my_group = lax.axis_index("samp")
    keep_count = picks.shape[0]
    phi = jnp.sqrt(jnp.float32(2.0)) * jnp.cos(
        jnp.dot(points, frequencies, preferred_element_type=jnp.float32) + phases[None, :]
    )
    signed = phi * signs.astype(jnp.float32)[:, None]
    mixed = jnp.dot(
        hadamard(rows), signed, precision=lax.Precision.HIGHEST, preferred_element_type=jnp.float32
    )
    for level in range(groups.bit_length() - 1):
        partner = partner_2(mixed, "samp", level)
        upper = jnp.bitwise_and(jnp.right_shift(my_group, level), 1) == 1
        mixed = jnp.where(upper, partner - mixed, mixed + partner)
    local_picks = picks - my_group * rows
    mixed = jnp.take(mixed, local_picks, axis=0)
    scale = 1.0 / float(keep_count * groups * rows * groups) ** 0.5
    chosen = (mixed * scale).astype(jnp.bfloat16)
    sketch_block = lax.all_gather(chosen, "samp", axis=0, tiled=True)
    ratio = groups // blocks
    columns = width // ratio
    offset = jnp.remainder(my_group, ratio) * columns
    own_slab = lax.dynamic_slice_in_dim(sketch_block, offset, columns, 1)
    slab = from_root(own_slab, "feat", my_group // ratio)
    return lax.dot_general(
        sketch_block, slab, (((0,), (0,)), ((), ())), preferred_element_type=jnp.float32
    )


def solution(mesh):
    return jax.shard_map(
        per_device,
        mesh=mesh,
        in_specs=(P("samp", None), P(None, "feat"), P("feat"), P("samp"), P("samp")),
        out_specs=P("feat", "samp"),
        check_vma=False,
    )
```

profile of v0, /device:TPU:6, one launch (start us, length us, event | category | flops | bytes accessed | tf_op | source)
XLA Modules:
  0.0 560.7 jit_solution(7349571527403986356)
XLA Ops:
  6.5 0.0 copy-start
  6.5 0.0 copy-start.2
  6.5 0.0 copy-start.3
  6.5 0.0 all-gather.2.cloned.1.call-start
  6.5 0.8 convert_multiply_fusion
  7.4 0.4 copy-done
  7.8 2.1 fusion.6
  9.9 0.0 copy-done.2
  9.9 0.0 copy-done.3
  9.9 42.2 %fusion = f32[512,4096]{1,0:T(8,128)} fusion(f32[512,512]{1,0:T(8,128)S(1)} %copy-done.2, f32[512,4096]{1,0:T(8,128)S(1)} %fusion.6, f32[512]{0:T(512)S(1)} %convert_multiply_fusion, f32[4096]{0:T(1024)S(1)} %copy-done.3), kind=kOutput, calls=%fused_computation.4 | convolution fusion | flops 12889096192 | bytes 17844224 | tf_op jit(solution)/shard_map/dot_general | solution.py:36
  52.1 0.0 collective-permute-start
  52.1 13.5 %collective-permute-done = f32[512,4096]{1,0:T(8,128)} collective-permute-done((f32[512,4096]{1,0:T(8,128)}, f32[512,4096]{1,0:T(8,128)}, u32[]{:S(2)}, u32[]{:S(2)}) %collective-permute-start) | collective-permute-done | bytes 8388640 | tf_op jit(solution)/shard_map/ppermute | solution.py:8
  65.6 11.7 %add_select_fusion.2 = f32[512,4096]{1,0:T(8,128)} fusion(f32[512,4096]{1,0:T(8,128)} %fusion, f32[512,4096]{1,0:T(8,128)} %collective-permute-done, pred[]{:T(512)S(6)} %eq.16), kind=kLoop, calls=%fused_computation.3 | loop fusion | flops 6291456 | bytes 25165824 | tf_op jit(solution)/shard_map/jit(_where)/select_n | solution.py:42
  77.3 0.5 collective-permute-start.1
  77.9 0.0 copy-start.4
  77.9 182.3 %collective-permute-done.1 = f32[512,4096]{1,0:T(8,128)} collective-permute-done((f32[512,4096]{1,0:T(8,128)}, f32[512,4096]{1,0:T(8,128)}, u32[]{:S(2)}, u32[]{:S(2)}) %collective-permute-start.1) | collective-permute-done | bytes 8388640 | tf_op jit(solution)/shard_map/ppermute | solution.py:8
  260.2 11.7 %add_select_fusion.1 = f32[512,4096]{1,0:T(8,128)} fusion(f32[512,4096]{1,0:T(8,128)} %add_select_fusion.2, f32[512,4096]{1,0:T(8,128)} %collective-permute-done.1, pred[]{:T(512)S(6)} %eq.15), kind=kLoop, calls=%fused_computation.2 | loop fusion | flops 6291456 | bytes 25165824 | tf_op jit(solution)/shard_map/jit(_where)/select_n | solution.py:42
  271.9 0.5 collective-permute-start.2
  272.4 0.0 copy-done.4
  272.4 181.4 %collective-permute-done.2 = f32[512,4096]{1,0:T(8,128)} collective-permute-done((f32[512,4096]{1,0:T(8,128)}, f32[512,4096]{1,0:T(8,128)}, u32[]{:S(2)}, u32[]{:S(2)}) %collective-permute-start.2) | collective-permute-done | bytes 8388640 | tf_op jit(solution)/shard_map/ppermute | solution.py:8
  453.8 11.7 %add_select_fusion = f32[512,4096]{1,0:T(8,128)} fusion(f32[512,4096]{1,0:T(8,128)} %add_select_fusion.1, f32[512,4096]{1,0:T(8,128)} %collective-permute-done.2, pred[]{:T(512)S(6)} %eq.14), kind=kLoop, calls=%fused_computation.1 | loop fusion | flops 6291456 | bytes 25165824 | tf_op jit(solution)/shard_map/jit(_where)/select_n | solution.py:42
  465.5 4.1 gather_fusion
  469.7 0.8 multiply_convert_fusion
  470.4 0.0 all-gather.2.cloned.1.call-update
  470.4 0.0 all-reduce.2.cloned.1.call-start
  470.5 23.7 %all-gather.2.cloned.1.call-done = bf16[128,4096]{1,0:T(8,128)(2,1)} async-done(((bf16[16,4096]{1,0:T(8,128)(2,1)}), bf16[128,4096]{1,0:T(8,128)(2,1)}) %all-gather.2.cloned.1.call-update) | async-done | bytes 1048592 | tf_op jit(solution)/shard_map/all_gather | solution.py:47
  494.2 1.9 dynamic-slice_select_fusion
  496.2 0.0 all-reduce.2.cloned.1.call-update
  496.2 40.0 %all-reduce.2.cloned.1.call-done = bf16[128,2048]{1,0:T(8,128)(2,1)} async-done(((bf16[128,2048]{1,0:T(8,128)(2,1)}), bf16[128,2048]{1,0:T(8,128)(2,1)}) %all-reduce.2.cloned.1.call-update) | async-done | bytes 524304 | tf_op jit(solution)/shard_map/psum | solution.py:13
  536.1 0.0 copy-start.1
  536.1 17.7 %fusion.7 = f32[4096,2048]{1,0:T(8,128)} fusion(bf16[128,4096]{1,0:T(8,128)(2,1)} %all-gather.2.cloned.1.call-done, bf16[128,2048]{1,0:T(8,128)(2,1)} %all-reduce.2.cloned.1.call-done), kind=kOutput, calls=%fused_computation.17 | convolution fusion | flops 2147483648 | bytes 35127296 | tf_op jit(solution)/shard_map/dot_general | solution.py:53
  553.8 0.0 copy-done.1
  (2 shorter events, 0.0 us)
Async XLA Ops:
  6.5 1.2 copy-start
  6.5 3.4 copy-start.2
  6.5 3.4 copy-start.3
  6.5 487.7 %all-gather.2.cloned.1.call-start = ((), (), s32[]{:S(2)}) async-start(), calls=%async_computation | async-start | bytes 1179648 | tf_op jit(solution)/shard_map/all_gather | solution.py:47
  52.1 13.5 %collective-permute-start = (f32[512,4096]{1,0:T(8,128)}, f32[512,4096]{1,0:T(8,128)}, u32[]{:S(2)}, u32[]{:S(2)}) collective-permute-start(f32[512,4096]{1,0:T(8,128)} %fusion), channel_id=1, source_target_pairs={{0,4},{4,0},{8,12},{12,8},{16,20},{20,16},{24,28},{28,24},{1,5},{5... | collective-permute-start | bytes 25165832 | tf_op jit(solution)/shard_map/ppermute | solution.py:8
  77.3 182.8 %collective-permute-start.1 = (f32[512,4096]{1,0:T(8,128)}, f32[512,4096]{1,0:T(8,128)}, u32[]{:S(2)}, u32[]{:S(2)}) collective-permute-start(f32[512,4096]{1,0:T(8,128)} %add_select_fusion.2), channel_id=1, source_target_pairs={{0,8},{4,12},{8,0},{12,4},{16,24},{20,28},{24,16},{28,20},{1,9},{5... | collective-permute-start | bytes 25165832 | tf_op jit(solution)/shard_map/ppermute | solution.py:8
  77.9 194.5 %copy-start.4 = (s32[16]{0:T(128)S(1)}, s32[16]{0:T(128)}, u32[]{:S(2)}) copy-start(s32[16]{0:T(128)} %param.9) | copy-start | bytes 196
  271.9 182.0 %collective-permute-start.2 = (f32[512,4096]{1,0:T(8,128)}, f32[512,4096]{1,0:T(8,128)}, u32[]{:S(2)}, u32[]{:S(2)}) collective-permute-start(f32[512,4096]{1,0:T(8,128)} %add_select_fusion.1), channel_id=1, source_target_pairs={{0,16},{4,20},{8,24},{12,28},{16,0},{20,4},{24,8},{28,12},{1,17},{... | collective-permute-start | bytes 25165832 | tf_op jit(solution)/shard_map/ppermute | solution.py:8
  470.4 65.7 %all-reduce.2.cloned.1.call-start = ((), (), s32[]{:S(2)}) async-start(), calls=%async_computation.1 | async-start | bytes 1048576 | tf_op jit(solution)/shard_map/psum | solution.py:13
  536.1 17.7 %copy-start.1 = (bf16[128,4096]{1,0:T(8,128)(2,1)S(1)}, bf16[128,4096]{1,0:T(8,128)(2,1)}, u32[]{:S(2)}) copy-start(bf16[128,4096]{1,0:T(8,128)(2,1)} %param.6) | copy-start | bytes 3145732
Sparse Core Ops, SparseCore 0:
  470.6 23.6 all-gather.1
  496.6 39.5 all-reduce.1
where the time goes:
time: 562 us; the launch traced here: 561 us
  waiting for transfers between devices  441 us (78%)
  matrix products  62 us (11%)
  other arithmetic  38.7 us (7%)
  between operations  13.5 us (2%)
    ppermute x3, waiting for transfers between devices, partner_2(): lax.ppermute(array, axis, [(i, i ^ 1 << distance) for i in range(lax.axis...  377 us
    dot_general x1, matrix products, per_device(): jnp.dot(hadamard(rows), signed, precision=lax.Precision.HIGHEST, preferre...  42.2 us
    psum x1, waiting for transfers between devices, from_root(): return lax.psum(kept, axis)  40 us
    select_n x3, other arithmetic, per_device(): mixed = jnp.where(upper, partner - mixed, mixed + partner)  35.1 us
    all_gather x1, waiting for transfers between devices, per_device(): sketch_block = lax.all_gather(chosen, 'samp', axis=0, tiled=True)  23.7 us
    dot_general x1, matrix products, per_device(): lax.dot_general(sketch_block, slab, (((0,), (0,)), ((), ())), preferred_e...  17.7 us
  transfers between devices with their start and end apart: 5, of which 5 were waited for; matrix products, arithmetic and copies ran while one was open for 0% of the time, Pallas kernels for 0%

commit v1 on v0

v1 whole, which is shorter than its diff:
```python
import functools

import jax
import jax.numpy as jnp
from jax import lax
from jax.experimental import pallas as pl
from jax.experimental.pallas import tpu as pltpu
from jax.sharding import PartitionSpec as P

MESH = pl.DeviceIdType.MESH
LANES = 128
SINE = (6.283185160089389, -41.34165503139731, 81.60100407217423, -76.54978227052618, 39.53670590280816)


def xor(a, b, bits):
    return sum(((a // 2**k + b // 2**k) % 2) * 2**k for k in range(bits))


def parity(value):
    for shift in (16, 8, 4, 2, 1):
        value = jnp.bitwise_xor(value, jnp.right_shift(value, shift))
    return jnp.bitwise_and(value, 1)


def flip(value):
    return 1.0 - 2.0 * parity(value).astype(jnp.float32)


def cosine(x):
    turns = x * 0.15915494309189535
    whole = (turns + 12582912.0) - 12582912.0
    y = 0.25 - jnp.abs(turns - whole)
    w = y * y
    p = w * SINE[4] + SINE[3]
    for c in SINE[2::-1]:
        p = p * w + c
    return p * y


def sketch_kernel(
    n, nf, scale, pts_ref, freq_ref, phase_ref, signs_ref, picks_ref, rows_ref, cols_ref,
    pts, sgn, pks, fbuf, pbuf, hloc, smat, acc,
    p_send, p_recv, p_fwd, s_send, s_recv, k_send, k_recv,
    r_send, r_recv, r_fwd, z_up, z_down, z_recv, local_sem,
):
    bits = n.bit_length() - 1
    me = lax.axis_index("samp")
    z = lax.axis_index("feat")
    core = me % 2
    mate = me + 1 - 2 * core
    rows = pts_ref.shape[0]
    fw = acc.shape[1]
    m = acc.shape[0]
    ratio = n // nf
    pieces = n // ratio
    root = me // ratio
    half = me % ratio

    loads = []
    if fw % LANES == 0:
        at = pl.multiple_of(me * fw, LANES)
        loads = [
            pltpu.make_async_copy(freq_ref.at[:, pl.ds(at, fw)], fbuf, local_sem.at[0]),
            pltpu.make_async_copy(phase_ref.at[:, pl.ds(at, fw)], pbuf, local_sem.at[1]),
        ]
    else:
        loads = [
            pltpu.make_async_copy(freq_ref, fbuf, local_sem.at[0]),
            pltpu.make_async_copy(phase_ref, pbuf, local_sem.at[1]),
        ]
    loads.append(pltpu.make_async_copy(pts_ref, pts.at[me], local_sem.at[2]))
    loads.append(pltpu.make_async_copy(signs_ref, sgn.at[me], local_sem.at[3]))
    loads.append(pltpu.make_async_copy(picks_ref, pks.at[me], local_sem.at[4]))
    for load in loads:
        load.start()

    barrier = pltpu.get_barrier_semaphore()
    for r in range(1, n):
        pl.semaphore_signal(barrier, inc=1, device_id={"samp": xor(me, r, bits)}, device_id_type=MESH)

    @pl.when(z + 1 < nf)
    def _():
        pl.semaphore_signal(barrier, inc=1, device_id={"feat": z + 1}, device_id_type=MESH)

    @pl.when(z > 0)
    def _():
        pl.semaphore_signal(barrier, inc=1, device_id={"feat": z - 1}, device_id_type=MESH)

    ends = jnp.where(z > 0, 1, 0) + jnp.where(z + 1 < nf, 1, 0)
    pl.semaphore_wait(barrier, n - 1 + ends)

    def remote(src, dst, send, recv, to):
        return pltpu.make_async_remote_copy(
            src_ref=src, dst_ref=dst, send_sem=send, recv_sem=recv, device_id=to, device_id_type=MESH
        )

    def small(r):
        peer = xor(me, r, bits)
        return (
            remote(picks_ref, pks.at[me], k_send.at[r], k_recv.at[me], {"samp": peer}),
            remote(signs_ref, sgn.at[me], s_send.at[r], s_recv.at[me], {"samp": peer}),
        )

    for r in range(1, n):
        for copy in small(r):
            copy.start()

    direct = [1] + list(range(2, n, 2))

    def own_points(r):
        return remote(pts_ref, pts.at[me], p_send.at[r], p_recv.at[me], {"samp": xor(me, r, bits)})

    for r in direct:
        own_points(r).start()

    def pass_points(src):
        return remote(pts.at[src], pts.at[src], p_fwd.at[src], p_recv.at[src], {"samp": mate})

    for load in loads:
        load.wait()
    for r in range(1, n):
        peer = xor(me, r, bits)
        remote(picks_ref, pks.at[peer], k_send.at[r], k_recv.at[peer], {"samp": peer}).wait_recv()

    picks = pks[...].reshape(m, LANES)
    lane = lax.broadcasted_iota(jnp.int32, (m, LANES), 1)
    for l in range(rows // LANES):
        hloc[:, l * LANES : (l + 1) * LANES] = flip(
            jnp.bitwise_and(jnp.bitwise_and(picks, rows - 1), lane + l * LANES)
        )
    acc[...] = jnp.zeros_like(acc)

    tile = min(rows, 256)

    def step(r, carry):
        src = xor(me, r, bits)

        @pl.when(r > 0)
        def _():
            remote(pts_ref, pts.at[src], p_send.at[r], p_recv.at[src], {"samp": mate}).wait_recv()
            remote(signs_ref, sgn.at[src], s_send.at[r], s_recv.at[src], {"samp": mate}).wait_recv()

        @pl.when(jnp.logical_and(r > 0, r % 2 == 0))
        def _():
            pass_points(src).start()

        group = flip(jnp.bitwise_and(pks[...].reshape(m, LANES), src * rows))
        for l in range(rows // LANES):
            s = slice(l * LANES, (l + 1) * LANES)
            smat[:, s] = (hloc[:, s] * (group * sgn[src, :, s].astype(jnp.float32))).astype(jnp.bfloat16)
        for k in range(rows // tile):
            s = slice(k * tile, (k + 1) * tile)
            x = jnp.dot(pts[src, s, :], fbuf[...], preferred_element_type=jnp.float32) + pbuf[...]
            c = cosine(x)
            hi = c.astype(jnp.bfloat16)
            lo = (c - hi.astype(jnp.float32)).astype(jnp.bfloat16)
            acc[...] += jnp.dot(smat[:, s], hi, preferred_element_type=jnp.float32) + jnp.dot(
                smat[:, s], lo, preferred_element_type=jnp.float32
            )
        return carry

    lax.fori_loop(0, n, step, 0)

    def part(g):
        return rows_ref.at[pl.ds(pl.multiple_of(g * fw, fw), fw), :]

    def slot(i):
        return cols_ref.at[pl.ds(pl.multiple_of(i * fw, fw), fw), :]

    rows_ref[pl.ds(pl.multiple_of(me * fw, fw), fw), :] = (acc[...] * scale).T.astype(jnp.bfloat16)

    def own_part(r):
        return remote(part(me), part(me), r_send.at[r], r_recv.at[me], {"samp": xor(me, r, bits)})

    for r in direct:
        own_part(r).start()

    def pass_part(src):
        return remote(part(src), part(src), r_fwd.at[src], r_recv.at[src], {"samp": mate})

    def up(src_ref, i):
        return remote(src_ref, slot(i), z_up.at[i], z_recv.at[i], {"feat": z + 1})

    def down(src_ref, i):
        return remote(src_ref, slot(i), z_down.at[i], z_recv.at[i], {"feat": z - 1})

    def exchange(r, carry):
        src = xor(me, r, bits)
        i = src % pieces

        @pl.when(r > 0)
        def _():
            remote(part(src), part(src), r_fwd.at[src], r_recv.at[src], {"samp": mate}).wait_recv()

        @pl.when(jnp.logical_and(r > 0, r % 2 == 0))
        def _():
            pass_part(src).start()

        mine = src // pieces == half

        @pl.when(jnp.logical_and(mine, z == root))
        def _():
            @pl.when(z + 1 < nf)
            def _():
                up(part(src), i).start()

            @pl.when(z > 0)
            def _():
                down(part(src), i).start()

            cols_ref[pl.ds(pl.multiple_of(i * fw, fw), fw), :] = rows_ref[
                pl.ds(pl.multiple_of(src * fw, fw), fw), :
            ]

        @pl.when(jnp.logical_and(mine, z != root))
        def _():
            remote(part(src), slot(i), z_up.at[i], z_recv.at[i], {"samp": mate}).wait_recv()

            @pl.when(jnp.logical_and(z > root, z + 1 < nf))
            def _():
                up(slot(i), i).start()

            @pl.when(jnp.logical_and(z < root, z > 0))
            def _():
                down(slot(i), i).start()

        return carry

    lax.fori_loop(0, n, exchange, 0)

    for r in range(1, n):
        for copy in small(r):
            copy.wait_send()
    for r in direct:
        own_points(r).wait_send()
        own_part(r).wait_send()
    for r in range(2, n, 2):
        src = xor(me, r, bits)
        pass_points(src).wait_send()
        pass_part(src).wait_send()
    for i in range(pieces):
        @pl.when(jnp.logical_and(z >= root, z + 1 < nf))
        def _():
            up(slot(i), i).wait_send()

        @pl.when(jnp.logical_and(z <= root, z > 0))
        def _():
            down(slot(i), i).wait_send()


def per_device(n, nf, points, frequencies, phases, signs, picks):
    rows, depth = points.shape
    width = frequencies.shape[1]
    keep = picks.shape[0]
    fw = width // n
    m = keep * n
    scale = (2.0 / float(m * rows * n)) ** 0.5
    phases = phases[None, :]
    if fw % LANES:
        at = lax.axis_index("samp") * fw
        frequencies = lax.dynamic_slice_in_dim(frequencies, at, fw, 1)
        phases = lax.dynamic_slice_in_dim(phases, at, fw, 1)
    columns = width * nf // n
    pieces = columns // fw
    vmem = pl.BlockSpec(memory_space=pltpu.VMEM)
    hbm = pl.BlockSpec(memory_space=pl.ANY)
    dma = pltpu.SemaphoreType.DMA
    block, slab = pl.pallas_call(
        functools.partial(sketch_kernel, n, nf, scale),
        out_shape=(
            jax.ShapeDtypeStruct((width, m), jnp.bfloat16),
            jax.ShapeDtypeStruct((columns, m), jnp.bfloat16),
        ),
        in_specs=[vmem, hbm, hbm, vmem, vmem],
        out_specs=(vmem, vmem),
        scratch_shapes=[
            pltpu.VMEM((n, rows, depth), jnp.bfloat16),
            pltpu.VMEM((n, 1, rows), jnp.int32),
            pltpu.VMEM((n, keep, LANES), jnp.int32),
            pltpu.VMEM((depth, fw), jnp.bfloat16),
            pltpu.VMEM((1, fw), jnp.float32),
            pltpu.VMEM((m, rows), jnp.float32),
            pltpu.VMEM((m, rows), jnp.bfloat16),
            pltpu.VMEM((m, fw), jnp.float32),
        ]
        + [dma((n,))] * 10
        + [dma((pieces,))] * 3
        + [dma((5,))],
        compiler_params=pltpu.CompilerParams(collective_id=0, has_side_effects=True),
    )(points, frequencies, phases, signs[None, :], jnp.broadcast_to(picks[:, None], (keep, LANES)))
    return lax.dot_general(
        block, slab, (((1,), (1,)), ((), ())), preferred_element_type=jnp.float32
    )


def solution(mesh):
    return jax.shard_map(
        functools.partial(per_device, mesh.shape["samp"], mesh.shape["feat"]),
        mesh=mesh,
        in_specs=(P("samp", None), P(None, "feat"), P("feat"), P("samp"), P("samp")),
        out_specs=P("feat", "samp"),
        check_vma=False,
    )
```

time: 562 us -> 64.4 us (0.11)
  waiting for transfers between devices: 441 us -> 0 us
  Pallas kernels: 0 us -> 45.4 us
  matrix products: 62 us -> 17.6 us
  other arithmetic: 38.7 us -> 0 us
  between operations: 13.5 us -> 0.01 us
    ppermute x3 -> x0, waiting for transfers between devices: 377 us -> none  [partner_2(): lax.ppermute(array, axis, [(i, i ^ 1 << distance) for i in range(lax.axis...]
    pallas_call x0 -> x1, Pallas kernels: none -> 45.4 us  [per_device(): pl.pallas_call(functools.partial(sketch_kernel, n, nf, scale), out_shape=...]
    dot_general x3 -> x1, matrix products: 62 us -> 17.6 us  [per_device(): lax.dot_general(block, slab, (((1,), (1,)), ((), ())), preferred_element_...]
    psum x1 -> x0, waiting for transfers between devices: 40 us -> none  [from_root(): return lax.psum(kept, axis)]
    select_n x4 -> x0, other arithmetic: 37.1 us -> none  [the longest x3 35.1 us: per_device(): mixed = jnp.where(upper, partner - mixed, mixed + partner)]
    all_gather x1 -> x0, waiting for transfers between devices: 23.7 us -> none  [per_device(): sketch_block = lax.all_gather(chosen, 'samp', axis=0, tiled=True)]
  transfers between devices with their start and end apart: 5 -> 0, of which waited for: 5 -> 0; matrix products, arithmetic and copies ran while one was open for 0% -> 0% of each run, Pallas kernels for 0% -> 0%
where the time goes in v1:
time: 64.4 us; the launch traced here: 64.3 us
  Pallas kernels  45.4 us (70%)
  matrix products  17.6 us (27%)
  local copies, waits for them, and re-layouts  1.32 us (2%)
    pallas_call x1, Pallas kernels, per_device(): pl.pallas_call(functools.partial(sketch_kernel, n, nf, scale), out_shape=...  45.4 us
    dot_general x1, matrix products, per_device(): lax.dot_general(block, slab, (((1,), (1,)), ((), ())), preferred_element_...  17.6 us
    broadcast_in_dim x1, local copies, waits for them, and re-layouts, per_device(): jnp.broadcast_to(picks[:, None], (keep, LANES))  1.32 us

profile of v1, /device:TPU:6, one launch (start us, length us, event | category | flops | bytes accessed | tf_op | source)
XLA Modules:
  0.0 64.3 jit_solution(10108117994694812922)
XLA Ops:
  0.0 1.3 %broadcast_in_dim.14.picks_ref = s32[16,128]{1,0:T(8,128)} broadcast(s32[16]{0:T(128)} %param.9), dimensions={0} | broadcast | bytes 8256 | tf_op jit(solution)/shard_map/broadcast_in_dim | solution.py:290
  1.3 45.4 %shard_map.55 = (bf16[4096,128]{1,0:T(8,128)(2,1)}, bf16[2048,128]{1,0:T(8,128)(2,1)}) custom-call(bf16[512,128]{1,0:T(8,128)(2,1)} %pts_ref.1, bf16[128,4096]{1,0:T(8,128)(2,1)} %freq_ref.1, f32[1,4096]{1,0:T(1,128)} %bitcast.4, s32[1,512]{1,0:T(1,128)} %bitcast.5, s32[16,128]{1,0:T(8,128)} %broadcast_in_dim.14.picks_ref), custom_call_target="tpu_custom_call" | custom-call | tf_op jit(solution)/shard_map/pallas_call | solution.py:268
  46.7 17.6 %fusion = f32[4096,2048]{1,0:T(8,128)} fusion(bf16[4096,128]{1,0:T(8,128)(2,1)} %get-tuple-element.7, bf16[2048,128]{1,0:T(8,128)(2,1)} %get-tuple-element.8), kind=kOutput, calls=%fused_computation | convolution fusion | flops 2147483648 | bytes 35127296 | tf_op jit(solution)/shard_map/dot_general | solution.py:291

commit v2 on v1

v2 whole, which is shorter than its diff:
```python
import functools

import jax
import jax.numpy as jnp
from jax import lax
from jax.experimental import pallas as pl
from jax.experimental.pallas import tpu as pltpu
from jax.sharding import PartitionSpec as P

MESH = pl.DeviceIdType.MESH
LANES = 128
NT = (((1,), (1,)), ((), ()))
SINE = (6.283185160089389, -41.34165503139731, 81.60100407217423, -76.54978227052618, 39.53670590280816)


def xor(a, b, bits):
    return sum(((a // 2**k + b // 2**k) % 2) * 2**k for k in range(bits))


def parity(value):
    for shift in (16, 8, 4, 2, 1):
        value = jnp.bitwise_xor(value, jnp.right_shift(value, shift))
    return jnp.bitwise_and(value, 1)


def flip(value):
    return 1.0 - 2.0 * parity(value).astype(jnp.float32)


def cosine(x):
    turns = x * 0.15915494309189535
    whole = (turns + 12582912.0) - 12582912.0
    y = 0.25 - jnp.abs(turns - whole)
    w = y * y
    p = w * SINE[4] + SINE[3]
    for c in SINE[2::-1]:
        p = p * w + c
    return p * y


class Gather:
    def __init__(self, me, mate, bits, own, block, send, recv):
        self.me, self.mate, self.bits = me, mate, bits
        self.own, self.block, self.send, self.recv = own, block, send, recv
        self.routes = []

    def copy(self, r, k, to, slot):
        src = xor(self.me, r, self.bits)
        here = self.own(k) if r == 0 else self.block(src, k)
        peer = self.mate if to == 1 else xor(self.me, to, self.bits)
        return pltpu.make_async_remote_copy(
            src_ref=here, dst_ref=self.block(src, k), send_sem=self.send.at[slot],
            recv_sem=self.recv.at[src, k], device_id={"samp": peer}, device_id_type=MESH,
        )

    def push(self, r, k, to):
        slot = len(self.routes)
        self.routes.append((r, k, to, slot))
        self.copy(r, k, to, slot).start()

    def start(self):
        for k in (0, 1):
            for b in range(1, self.bits):
                self.push(0, k if b == 1 else 1 - k, 1 << b)
        for k in (0, 1):
            self.push(0, k, 1)

    def arrive(self, r):
        for k in (0, 1):
            self.copy(r, k, 1, 0).wait_recv()
            if r % 2 == 0:
                q = r // 2
                top, low = q.bit_length() - 1, (q & -q).bit_length() - 1
                onward = range(top + 1, self.bits - 1) if k == 0 else range(low)
                for b in onward:
                    self.push(r, k, 2 << b)
                self.push(r, k, 1)

    def finish(self):
        for route in self.routes:
            self.copy(*route).wait_send()


def sends(n):
    bits = n.bit_length() - 1
    count = 2 * bits
    for r in range(2, n, 2):
        q = r // 2
        count += 2 + bits - 1 - q.bit_length() + (q & -q).bit_length() - 1
    return count


def sketch_kernel(
    n, nf, scale, pts_ref, freq_ref, phase_ref, signs_ref, picks_ref, rows_ref, cols_ref,
    pts, sgn, pks, fbuf, pbuf, hloc, smat, acc, ftr, ptr, wide,
    p_send, p_recv, s_send, s_recv, k_send, k_recv,
    r_send, r_recv, z_up, z_down, z_recv, local_sem,
):
    bits = n.bit_length() - 1
    me = lax.axis_index("samp")
    z = lax.axis_index("feat")
    core = me % 2
    mate = me + 1 - 2 * core
    rows = pts_ref.shape[0]
    fw = acc.shape[0]
    m = acc.shape[1]
    ratio = n // nf
    pieces = n // ratio
    root = me // ratio
    half = me % ratio

    loads = []
    if fw % LANES == 0:
        at = pl.multiple_of(me * fw, LANES)
        loads = [
            pltpu.make_async_copy(freq_ref.at[:, pl.ds(at, fw)], fbuf, local_sem.at[0]),
            pltpu.make_async_copy(phase_ref.at[:, pl.ds(at, fw)], pbuf, local_sem.at[1]),
        ]
    else:
        loads = [
            pltpu.make_async_copy(freq_ref, fbuf, local_sem.at[0]),
            pltpu.make_async_copy(phase_ref, pbuf, local_sem.at[1]),
        ]
    loads.append(pltpu.make_async_copy(pts_ref, pts.at[me], local_sem.at[2]))
    loads.append(pltpu.make_async_copy(signs_ref, sgn.at[me], local_sem.at[3]))
    loads.append(pltpu.make_async_copy(picks_ref, pks.at[me], local_sem.at[4]))
    for load in loads:
        load.start()

    barrier = pltpu.get_barrier_semaphore()
    for r in range(1, n):
        pl.semaphore_signal(barrier, inc=1, device_id={"samp": xor(me, r, bits)}, device_id_type=MESH)

    @pl.when(z + 1 < nf)
    def _():
        pl.semaphore_signal(barrier, inc=1, device_id={"feat": z + 1}, device_id_type=MESH)

    @pl.when(z > 0)
    def _():
        pl.semaphore_signal(barrier, inc=1, device_id={"feat": z - 1}, device_id_type=MESH)

    ends = jnp.where(z > 0, 1, 0) + jnp.where(z + 1 < nf, 1, 0)
    pl.semaphore_wait(barrier, n - 1 + ends)

    def remote(src, dst, send, recv, to):
        return pltpu.make_async_remote_copy(
            src_ref=src, dst_ref=dst, send_sem=send, recv_sem=recv, device_id=to, device_id_type=MESH
        )

    def small(r):
        peer = xor(me, r, bits)
        return (
            remote(picks_ref, pks.at[me], k_send.at[r], k_recv.at[me], {"samp": peer}),
            remote(signs_ref, sgn.at[me], s_send.at[r], s_recv.at[me], {"samp": peer}),
        )

    for r in range(1, n):
        for copy in small(r):
            copy.start()

    half_width = fw // 2
    near = [1 << b for b in range(1, bits)]
    far = [r for r in range(2, n, 2) if r not in near]
    halved = rows // 2
    points = Gather(
        me, mate, bits, lambda k: pts_ref.at[pl.ds(k * halved, halved), :],
        lambda g, k: pts.at[g, pl.ds(k * halved, halved), :], p_send, p_recv,
    )
    points.start()

    for load in loads:
        load.wait()
    for r in range(1, n):
        peer = xor(me, r, bits)
        remote(picks_ref, pks.at[peer], k_send.at[r], k_recv.at[peer], {"samp": peer}).wait_recv()

    keep = picks_ref.shape[1]
    eye = lax.broadcasted_iota(jnp.int32, (keep, keep), 0) == lax.broadcasted_iota(jnp.int32, (keep, keep), 1)
    for g in range(n):
        line = jnp.broadcast_to(pks[g].astype(jnp.float32), (keep, keep))
        column = jnp.sum(jnp.where(eye, line, 0.0), axis=1, keepdims=True)
        wide[g * keep : (g + 1) * keep, :] = jnp.broadcast_to(column, (keep, LANES)).astype(jnp.int32)
    picks = wide[...]
    lane = lax.broadcasted_iota(jnp.int32, (m, LANES), 1)
    for l in range(rows // LANES):
        hloc[:, l * LANES : (l + 1) * LANES] = flip(
            jnp.bitwise_and(jnp.bitwise_and(picks, rows - 1), lane + l * LANES)
        )
    acc[...] = jnp.zeros_like(acc)

    tile = min(fw, 256)
    ftr[...] = fbuf[...].astype(jnp.float32).T.astype(jnp.bfloat16)
    ptr[...] = jnp.broadcast_to(pbuf[...], (8, fw)).T[:, :1]

    def step(r, carry):
        src = xor(me, r, bits)

        for q in range(1, n):
            @pl.when(r == q)
            def _(q=q):
                for first in near if q == 2 else [] if q in near else [q]:
                    points.arrive(first)

        @pl.when(r > 0)
        def _():
            remote(signs_ref, sgn.at[src], s_send.at[r], s_recv.at[src], {"samp": mate}).wait_recv()

        group = flip(jnp.bitwise_and(wide[...], src * rows))
        for l in range(rows // LANES):
            s = slice(l * LANES, (l + 1) * LANES)
            smat[:, s] = (hloc[:, s] * (group * sgn[src, :, s].astype(jnp.float32))).astype(jnp.bfloat16)
        for k in range(fw // tile):
            s = slice(k * tile, (k + 1) * tile)
            x = lax.dot_general(ftr[s, :], pts[src], NT, preferred_element_type=jnp.float32) + ptr[s, :]
            c = cosine(x)
            hi = c.astype(jnp.bfloat16)
            lo = (c - hi.astype(jnp.float32)).astype(jnp.bfloat16)
            acc[s, :] += lax.dot_general(hi, smat[...], NT, preferred_element_type=jnp.float32) + lax.dot_general(
                lo, smat[...], NT, preferred_element_type=jnp.float32
            )
        return carry

    lax.fori_loop(0, n, step, 0)

    def part(g, k):
        return rows_ref.at[pl.ds(pl.multiple_of(g * fw + k * half_width, half_width), half_width), :]

    def slot(i, k):
        return cols_ref.at[pl.ds(pl.multiple_of(i * fw + k * half_width, half_width), half_width), :]

    rows_ref[pl.ds(pl.multiple_of(me * fw, fw), fw), :] = (acc[...] * scale).astype(jnp.bfloat16)

    parts = Gather(me, mate, bits, lambda k: part(me, k), part, r_send, r_recv)
    parts.start()

    def up(src_ref, i, k):
        return remote(src_ref, slot(i, k), z_up.at[i, k], z_recv.at[i, k], {"feat": z + 1})

    def down(src_ref, i, k):
        return remote(src_ref, slot(i, k), z_down.at[i, k], z_recv.at[i, k], {"feat": z - 1})

    def along(r):
        src = xor(me, r, bits)
        i = src % pieces
        mine = src // pieces == half

        @pl.when(jnp.logical_and(mine, z == root))
        def _():
            @pl.when(z + 1 < nf)
            def _():
                for k in (0, 1):
                    up(part(src, k), i, k).start()

            @pl.when(z > 0)
            def _():
                for k in (0, 1):
                    down(part(src, k), i, k).start()

            cols_ref[pl.ds(pl.multiple_of(i * fw, fw), fw), :] = rows_ref[
                pl.ds(pl.multiple_of(src * fw, fw), fw), :
            ]

        @pl.when(jnp.logical_and(mine, z != root))
        def _():
            for k in (0, 1):
                remote(part(src, k), slot(i, k), z_up.at[i, k], z_recv.at[i, k], {"samp": mate}).wait_recv()

                @pl.when(jnp.logical_and(z > root, z + 1 < nf))
                def _():
                    up(slot(i, k), i, k).start()

                @pl.when(jnp.logical_and(z < root, z > 0))
                def _():
                    down(slot(i, k), i, k).start()

    parts.arrive(1)
    for r in near:
        parts.arrive(r)
    for r in [0, 1] + near:
        along(r)
    for r in near:
        parts.arrive(r + 1)
        along(r + 1)
    for r in far:
        parts.arrive(r)
        along(r)
        parts.arrive(r + 1)
        along(r + 1)

    for r in range(1, n):
        for copy in small(r):
            copy.wait_send()
    points.finish()
    parts.finish()
    for i, k in [(i, k) for i in range(pieces) for k in (0, 1)]:
        @pl.when(jnp.logical_and(z >= root, z + 1 < nf))
        def _():
            up(slot(i, k), i, k).wait_send()

        @pl.when(jnp.logical_and(z <= root, z > 0))
        def _():
            down(slot(i, k), i, k).wait_send()


def gram_kernel(a_ref, b_ref, o_ref):
    tall = min(o_ref.shape[0], 1024)
    for i in range(o_ref.shape[0] // tall):
        s = slice(i * tall, (i + 1) * tall)
        o_ref[s, :] = lax.dot_general(
            a_ref[s, :], b_ref[...], NT, preferred_element_type=jnp.float32
        )


def gram(block, slab):
    tall, m = block.shape
    wide = slab.shape[0]
    step = min(wide, 256)
    return pl.pallas_call(
        gram_kernel,
        out_shape=jax.ShapeDtypeStruct((tall, wide), jnp.float32),
        grid=(wide // step,),
        in_specs=[pl.BlockSpec((tall, m), lambda j: (0, 0)), pl.BlockSpec((step, m), lambda j: (j, 0))],
        out_specs=pl.BlockSpec((tall, step), lambda j: (0, j)),
    )(block, slab)


def per_device(n, nf, points, frequencies, phases, signs, picks):
    rows, depth = points.shape
    width = frequencies.shape[1]
    keep = picks.shape[0]
    fw = width // n
    m = keep * n
    scale = (2.0 / float(m * rows * n)) ** 0.5
    phases = phases[None, :]
    if fw % LANES:
        at = lax.axis_index("samp") * fw
        frequencies = lax.dynamic_slice_in_dim(frequencies, at, fw, 1)
        phases = lax.dynamic_slice_in_dim(phases, at, fw, 1)
    columns = width * nf // n
    pieces = columns // fw
    vmem = pl.BlockSpec(memory_space=pltpu.VMEM)
    hbm = pl.BlockSpec(memory_space=pl.ANY)
    dma = pltpu.SemaphoreType.DMA
    block, slab = pl.pallas_call(
        functools.partial(sketch_kernel, n, nf, scale),
        out_shape=(
            jax.ShapeDtypeStruct((width, m), jnp.bfloat16),
            jax.ShapeDtypeStruct((columns, m), jnp.bfloat16),
        ),
        in_specs=[vmem, hbm, hbm, vmem, vmem],
        out_specs=(vmem, vmem),
        scratch_shapes=[
            pltpu.VMEM((n, rows, depth), jnp.bfloat16),
            pltpu.VMEM((n, 1, rows), jnp.int32),
            pltpu.VMEM((n, 1, keep), jnp.int32),
            pltpu.VMEM((depth, fw), jnp.bfloat16),
            pltpu.VMEM((1, fw), jnp.float32),
            pltpu.VMEM((m, rows), jnp.float32),
            pltpu.VMEM((m, rows), jnp.bfloat16),
            pltpu.VMEM((fw, m), jnp.float32),
            pltpu.VMEM((fw, depth), jnp.bfloat16),
            pltpu.VMEM((fw, 1), jnp.float32),
            pltpu.VMEM((m, LANES), jnp.int32),
        ]
        + [dma((sends(n),)), dma((n, 2))]
        + [dma((n,))] * 4
        + [dma((sends(n),)), dma((n, 2))]
        + [dma((pieces, 2))] * 3
        + [dma((5,))],
        compiler_params=pltpu.CompilerParams(collective_id=0, has_side_effects=True),
    )(points, frequencies, phases, signs[None, :], picks[None, :])
    return gram(block, slab)


def solution(mesh):
    return jax.shard_map(
        functools.partial(per_device, mesh.shape["samp"], mesh.shape["feat"]),
        mesh=mesh,
        in_specs=(P("samp", None), P(None, "feat"), P("feat"), P("samp"), P("samp")),
        out_specs=P("feat", "samp"),
        check_vma=False,
    )
```

time: 64.4 us -> 58.4 us (0.907)
  matrix products: 17.6 us -> 0 us
  Pallas kernels: 45.4 us -> 58.2 us
  local copies, waits for them, and re-layouts: 1.32 us -> 0 us
    dot_general x1 -> x0, matrix products: 17.6 us -> none  [per_device(): lax.dot_general(block, slab, (((1,), (1,)), ((), ())), preferred_element_...]
    pallas_call x0 -> x1, Pallas kernels: none -> 13.5 us  [gram(): pl.pallas_call(gram_kernel, out_shape=jax.ShapeDtypeStruct((tall, wide),...]
    broadcast_in_dim x1 -> x0, local copies, waits for them, and re-layouts: 1.32 us -> none  [per_device(): jnp.broadcast_to(picks[:, None], (keep, LANES))]
    pallas_call x1, Pallas kernels: 45.4 us -> 44.7 us  [per_device(): pl.pallas_call(functools.partial(sketch_kernel, n, nf, scale), out_shape=...]
where the time goes in v2:
time: 58.4 us; the launch traced here: 58.2 us
  Pallas kernels  58.2 us (100%)
    pallas_call x1, Pallas kernels, per_device(): pl.pallas_call(functools.partial(sketch_kernel, n, nf, scale), out_shape=...  44.7 us
    pallas_call x1, Pallas kernels, gram(): pl.pallas_call(gram_kernel, out_shape=jax.ShapeDtypeStruct((tall, wide),...  13.5 us

profile of v2, /device:TPU:6, one launch (start us, length us, event | category | flops | bytes accessed | tf_op | source)
XLA Modules:
  0.0 58.2 jit_solution(17771164303438509576)
XLA Ops:
  0.0 44.7 %shard_map.55 = (bf16[4096,128]{1,0:T(8,128)(2,1)}, bf16[2048,128]{1,0:T(8,128)(2,1)}) custom-call(bf16[512,128]{1,0:T(8,128)(2,1)} %pts_ref.1, bf16[128,4096]{1,0:T(8,128)(2,1)} %freq_ref.1, f32[1,4096]{1,0:T(1,128)} %bitcast.3, s32[1,512]{1,0:T(1,128)} %bitcast.4, s32[1,16]{1,0:T(1,128)} %bitcast.5), custom_call_target="tpu_custom_call" | custom-call | tf_op jit(solution)/shard_map/pallas_call | solution.py:344
  44.7 13.5 %shard_map.56 = f32[4096,2048]{1,0:T(8,128)} custom-call(bf16[4096,128]{1,0:T(8,128)(2,1)} %get-tuple-element.7.a_ref, bf16[2048,128]{1,0:T(8,128)(2,1)} %get-tuple-element.8.b_ref), custom_call_target="tpu_custom_call" | custom-call | tf_op jit(solution)/shard_map/pallas_call | solution.py:318
